TPU v7x, 32 devices: a whole 2x2x4 slice. The times are simulated.
32 devices in a mesh: tm: 4 (over y, x), rows: 8 (over z, core).
Axes of the slice: x: 2, y: 2, z: 4, core: 2. Of those that a mesh axis runs over, the one named last changes fastest.
Arguments:
- features: bfloat16 [48, 1280, 512], P('rows', 'tm'), may hold values from -6 to 6
- cotangent: bfloat16 [48, 1280, 512], P('rows', 'tm'), may hold values from -6 to 6
- state_bank: float32 [48, 512, 32], P('rows', 'tm'), may hold values from -6 to 6
- state_source: int32 [48], P('rows'), may hold values from 0 to 5, as said below
- master: float32 [88, 256, 256], P('tm', 'rows'), may hold values from -0.13258252 to 0.13258252
- left_stats: float32 [88, 256, 256], P('tm', 'rows'), may hold values from -7.68 to 64
- right_stats: float32 [88, 256, 256], P('tm', 'rows'), may hold values from -7.68 to 64
- left_root: float32 [88, 256, 256], P('tm', 'rows'), may hold values from -0.2 to 1.6
- right_root: float32 [88, 256, 256], P('tm'), may hold values from -0.2 to 1.6
- small_params: float32 [20, 512], replicated, may hold values from -1 to 1.5
- decay_logs: float32 [8, 32], P('tm'), may hold values from -7 to -1.5
- state_mix: float32 [2, 512, 32], P(None, 'tm'), may hold values from -0.6 to 0.6
Outputs:
- layer_out: bfloat16 [48, 1280, 512], P('rows', 'tm')
- grad_features: float32 [48, 1280, 512], P('rows', 'tm')
- grad_state: float32 [48, 512, 32], P('rows', 'tm')
- grad_blocks: float32 [88, 256, 256], P('tm', 'rows')
- new_left: float32 [88, 256, 256], P('tm', 'rows')
- new_right: float32 [88, 256, 256], P('tm', 'rows')
- new_master: float32 [88, 256, 256], P('tm', 'rows')
- new_copy: bfloat16 [88, 256, 256], P('tm', 'rows')
- grad_small: float32 [20, 512], P(None, 'tm')
- new_small: float32 [20, 512], P(None, 'tm')
- grad_decay: float32 [8, 32], P('tm')
- grad_mix: float32 [2, 512, 32], P(None, 'tm')
- new_decay: float32 [8, 32], P('tm')
- new_mix: float32 [2, 512, 32], P(None, 'tm')
Inputs may be any that keep to these rules, and one draw needn't show every extreme that they name: `state_source`: within each aligned block of 6 rows the values are a permutation of 0 to 5.
All inputs are finite; a program needn't handle non-finite values.
Results may differ from a plain program's by a relative error of at most 0.018.
Values may be sent and summed in bfloat16 or wider, within the bound.
A program may use at most 320 MiB of HBM per device.

v0:
```python
from functools import partial
import math
import jax
import jax.numpy as jnp
from jax import lax
from jax.sharding import PartitionSpec as P

D = 512
FF = 2048
NST = 32
KW = 15
BS = 256
precise = lax.Precision.HIGHEST
three_pass = lax.Precision.HIGH
rate_blocks = 0.1
rate_small = 0.5


def with_halo(block, sides, width):
    for axis, dim in sides:
        count = lax.axis_size(axis)
        forward = [(i, i + 1) for i in range(count - 1)]
        backward = [(target, source) for source, target in forward]
        low = lax.ppermute(
            lax.slice_in_dim(block, block.shape[dim] - width, None, axis=dim), axis, forward
        )
        high = lax.ppermute(lax.slice_in_dim(block, 0, width, axis=dim), axis, backward)
        block = jnp.concatenate([low, block, high], axis=dim)
    return block


def layer_norm(values, scales):
    center = values - jnp.mean(values, axis=-1, keepdims=True)
    spread = jnp.mean(center * center, axis=-1, keepdims=True)
    return center * lax.rsqrt(spread + 1e-05) * scales


def norm_back(values, scales, incoming):
    unused, pull_back = jax.vjp(layer_norm, values, scales)
    return pull_back(incoming)


def gating(values):
    half_width = values.shape[-1] // 2
    return values[..., :half_width] * jax.nn.sigmoid(values[..., half_width:])


def silu_back(values, incoming):
    return jax.vjp(jax.nn.silu, values)[1](incoming)[0]


def gating_back(values, incoming):
    return jax.vjp(gating, values)[1](incoming)[0]


def matmul(first, second):
    return jnp.dot(first, second, preferred_element_type=jnp.float32)


def inner_rows(first, second):
    return lax.dot_general(
        first, second, (((0,), (0,)), ((), ())), preferred_element_type=jnp.float32
    )


def inner_cols(first, second):
    return lax.dot_general(
        first, second, (((1,), (1,)), ((), ())), preferred_element_type=jnp.float32
    )


def to_matrix(block_stack, first, rows_count, cols_count):
    blocks_down = rows_count // BS
    blocks_across = cols_count // BS
    picked = block_stack[first : first + blocks_down * blocks_across]
    picked = picked.reshape(blocks_down, blocks_across, BS, BS).transpose(0, 2, 1, 3)
    return picked.reshape(rows_count, cols_count)


def to_blocks(matrix):
    rows_count, cols_count = matrix.shape
    return (
        matrix.reshape(rows_count // BS, BS, cols_count // BS, BS)
        .transpose(0, 2, 1, 3)
        .reshape(-1, BS, BS)
    )


def matrices(block_stack):
    ffn_count = D // BS * (FF // BS)
    mix_count = (D // BS) ** 2
    base_index = 4 * ffn_count
    return (
        to_matrix(block_stack, 0, D, FF),
        to_matrix(block_stack, ffn_count, FF, D),
        to_matrix(block_stack, 2 * ffn_count, D, FF),
        to_matrix(block_stack, 3 * ffn_count, FF, D),
        to_matrix(block_stack, base_index, D, D),
        to_matrix(block_stack, base_index + mix_count, D, 2 * D),
        to_matrix(block_stack, base_index + 3 * mix_count, D, 2 * D),
        to_matrix(block_stack, base_index + 5 * mix_count, D, D),
    )


def dft_tables(frames):
    period = 2 * frames - 1
    counter = jnp.arange(frames, dtype=jnp.int32)
    phase = (counter[:, None] * counter[None, :] % period).astype(jnp.float32) * (
        2.0 * math.pi / period
    )
    cosine = jnp.cos(phase)
    sine = jnp.sin(phase)
    forward_table = jnp.concatenate([cosine, -sine], axis=1)
    table_high = forward_table.astype(jnp.bfloat16)
    table_rest = (forward_table - table_high.astype(jnp.float32)).astype(jnp.bfloat16)
    split_table = jnp.concatenate([table_high, table_rest], axis=1)
    weighting = jnp.where(counter == 0, 1.0, 2.0).astype(jnp.float32) / period
    inverse_table = jnp.concatenate(
        [cosine * weighting[:, None], -sine * weighting[:, None]], axis=0
    )
    return (forward_table, split_table, inverse_table)


def conv_local(
    inputs_here,
    bank_rows,
    log_rates,
    mix_terms,
    selector,
    forward_table,
    split_table,
    inverse_table,
):
    row_count, frames, width = inputs_here.shape
    head_count = log_rates.shape[0]
    decay_rates = jnp.exp(log_rates)
    positions = jnp.arange(frames, dtype=jnp.float32)
    decay_now = jnp.exp(-decay_rates[:, :, None] * positions)
    decay_next = jnp.exp(-decay_rates[:, :, None] * (positions + 1.0))
    coupling = (mix_terms[0] * mix_terms[1]).reshape(head_count, width // head_count, NST)
    kernel = jnp.einsum("hdn,hnt->hdt", coupling, decay_now, precision=precise).reshape(
        width, frames
    )
    kernel_hat = jnp.dot(kernel, forward_table, precision=precise)
    both_hat = jnp.einsum(
        "rtc,tk->rck",
        inputs_here.astype(jnp.bfloat16),
        split_table,
        preferred_element_type=jnp.float32,
    )
    input_hat = both_hat[..., : 2 * frames] + both_hat[..., 2 * frames :]
    real_in = input_hat[..., :frames]
    imag_in = input_hat[..., frames:]
    real_kernel = kernel_hat[:, :frames]
    imag_kernel = kernel_hat[:, frames:]
    output_hat = jnp.concatenate(
        [
            real_in * real_kernel - imag_in * imag_kernel,
            real_in * imag_kernel + imag_in * real_kernel,
        ],
        axis=-1,
    )
    mixed = jnp.einsum("rck,kt->rtc", output_hat, inverse_table, precision=three_pass)
    starts = jnp.einsum("rs,scn->rcn", selector, bank_rows, precision=precise)
    carried = (mix_terms[1][None] * starts).reshape(row_count, head_count, width // head_count, NST)
    carried_out = jnp.einsum("rhdn,hnt->rthd", carried, decay_next, precision=precise)
    return mixed + carried_out.reshape(row_count, frames, width)


def ffn_forward(values, scales, weight_in, weight_out):
    normed = layer_norm(values, scales).astype(jnp.bfloat16)
    inner = matmul(normed, weight_in)
    activated = jax.nn.silu(inner).astype(jnp.bfloat16)
    return (0.5 * matmul(activated, weight_out), (normed, inner, activated))


def ffn_backward(values, scales, weight_in, weight_out, saved, incoming):
    normed, inner, activated = saved
    grad_outer = (0.5 * incoming).astype(jnp.bfloat16)
    grad_weight_out = inner_rows(activated, grad_outer)
    grad_act = inner_cols(grad_outer, weight_out)
    grad_inner = silu_back(inner, grad_act).astype(jnp.bfloat16)
    grad_weight_in = inner_rows(normed, grad_inner)
    grad_normed = inner_cols(grad_inner, weight_in)
    grad_values, grad_scales = norm_back(values, scales, grad_normed)
    return (incoming + grad_values, grad_scales, grad_weight_in, grad_weight_out)


def body(
    features,
    cotangent,
    state_bank,
    state_source,
    master,
    left_stats,
    right_stats,
    left_root,
    right_root,
    small_params,
    decay_logs,
    state_mix,
):
    row_count, frame_count, width = features.shape
    token_count = row_count * frame_count
    margin = (KW - 1) // 2
    scaling = 1.0 / math.sqrt(token_count * lax.axis_size("tm") * lax.axis_size("rows"))
    copy_part = master.astype(jnp.bfloat16)
    partial_stack = lax.all_gather(copy_part, "rows", axis=1, tiled=True)
    block_stack = lax.all_gather(partial_stack, "tm", axis=0, tiled=True)
    ffa_in, ffa_out, ffb_in, ffb_out, mixer_in, mixer_out, conv_in, conv_out = matrices(block_stack)
    kernel_rows = small_params[5:]
    stream_zero = features.astype(jnp.float32).reshape(token_count, width)
    branch_one, saved_one = ffn_forward(stream_zero, small_params[0], ffa_in, ffa_out)
    stream_one = stream_zero + branch_one
    normed_mixer = layer_norm(stream_one, small_params[1]).astype(jnp.bfloat16)
    mixer_input = (
        matmul(normed_mixer, mixer_in).astype(jnp.bfloat16).reshape(row_count, frame_count, width)
    )
    channel_in = lax.all_to_all(mixer_input, "tm", split_axis=2, concat_axis=1, tiled=True)
    forward_table, split_table, inverse_table = dft_tables(channel_in.shape[1])
    selector = (state_source[:, None] == jnp.arange(row_count, dtype=jnp.int32)[None, :]).astype(
        jnp.float32
    )
    mixer_local = partial(
        conv_local,
        selector=selector,
        forward_table=forward_table,
        split_table=split_table,
        inverse_table=inverse_table,
    )
    channel_out, mixer_pull = jax.vjp(
        mixer_local, channel_in.astype(jnp.float32), state_bank, decay_logs, state_mix
    )
    mixer_result = lax.all_to_all(
        channel_out.astype(jnp.bfloat16), "tm", split_axis=1, concat_axis=2, tiled=True
    ).reshape(token_count, width)
    gated = matmul(mixer_result, mixer_out)
    stream_two = stream_one + gating(gated)
    normed_conv = layer_norm(stream_two, small_params[2]).astype(jnp.bfloat16)
    pointwise = matmul(normed_conv, conv_in)
    gated_units = gating(pointwise).astype(jnp.bfloat16).reshape(row_count, frame_count, width)
    padded = with_halo(gated_units, (("tm", 1),), margin)
    padded_full = padded.astype(jnp.float32)
    depthwise = kernel_rows[0] * padded_full[:, 0:frame_count]
    for offset in range(1, KW):
        depthwise = depthwise + kernel_rows[offset] * padded_full[:, offset : offset + frame_count]
    depth_flat = depthwise.reshape(token_count, width)
    activated_conv = jax.nn.silu(depth_flat).astype(jnp.bfloat16)
    stream_three = stream_two + matmul(activated_conv, conv_out)
    branch_four, saved_four = ffn_forward(stream_three, small_params[3], ffb_in, ffb_out)
    stream_four = stream_three + branch_four
    layer_out, out_pull = jax.vjp(layer_norm, stream_four, small_params[4])
    grad_four, grad_gain_out = out_pull(cotangent.astype(jnp.float32).reshape(token_count, width))
    grad_three, grad_gain_b, grad_fb_in, grad_fb_out = ffn_backward(
        stream_three, small_params[3], ffb_in, ffb_out, saved_four, grad_four
    )
    grad_conv_out = grad_three.astype(jnp.bfloat16)
    grad_weight_conv_out = inner_rows(activated_conv, grad_conv_out)
    grad_activated = inner_cols(grad_conv_out, conv_out)
    grad_depth = (
        silu_back(depth_flat, grad_activated)
        .astype(jnp.bfloat16)
        .reshape(row_count, frame_count, width)
    )
    grad_padded = with_halo(grad_depth, (("tm", 1),), margin).astype(jnp.float32)
    grad_depth_full = grad_depth.astype(jnp.float32)
    grad_units = kernel_rows[0] * grad_padded[:, 2 * margin : 2 * margin + frame_count]
    kernel_grads = [jnp.sum(grad_depth_full * padded_full[:, 0:frame_count], axis=(0, 1))]
    for offset in range(1, KW):
        grad_units = (
            grad_units
            + kernel_rows[offset]
            * grad_padded[:, 2 * margin - offset : 2 * margin - offset + frame_count]
        )
        kernel_grads.append(
            jnp.sum(grad_depth_full * padded_full[:, offset : offset + frame_count], axis=(0, 1))
        )
    grad_pointwise = gating_back(pointwise, grad_units.reshape(token_count, width)).astype(
        jnp.bfloat16
    )
    grad_weight_conv_in = inner_rows(normed_conv, grad_pointwise)
    grad_values, grad_gain_c = norm_back(
        stream_two, small_params[2], inner_cols(grad_pointwise, conv_in)
    )
    grad_two = grad_three + grad_values
    grad_gated = gating_back(gated, grad_two).astype(jnp.bfloat16)
    grad_weight_mixer_out = inner_rows(mixer_result, grad_gated)
    grad_mixer_frames = (
        inner_cols(grad_gated, mixer_out)
        .astype(jnp.bfloat16)
        .reshape(row_count, frame_count, width)
    )
    grad_channel_out = lax.all_to_all(
        grad_mixer_frames, "tm", split_axis=2, concat_axis=1, tiled=True
    )
    grad_channel_in, grad_state, grad_logs, grad_mix_terms = mixer_pull(
        grad_channel_out.astype(jnp.float32)
    )
    grad_input_frames = lax.all_to_all(
        grad_channel_in.astype(jnp.bfloat16), "tm", split_axis=1, concat_axis=2, tiled=True
    ).reshape(token_count, width)
    grad_weight_mixer_in = inner_rows(normed_mixer, grad_input_frames)
    grad_values, grad_gain_s = norm_back(
        stream_one, small_params[1], inner_cols(grad_input_frames, mixer_in)
    )
    grad_one = grad_two + grad_values
    grad_zero, grad_gain_a, grad_fa_in, grad_fa_out = ffn_backward(
        stream_zero, small_params[0], ffa_in, ffa_out, saved_one, grad_one
    )
    grad_stack = (
        jnp.concatenate(
            [
                to_blocks(grad_fa_in),
                to_blocks(grad_fa_out),
                to_blocks(grad_fb_in),
                to_blocks(grad_fb_out),
                to_blocks(grad_weight_mixer_in),
                to_blocks(grad_weight_mixer_out),
                to_blocks(grad_weight_conv_in),
                to_blocks(grad_weight_conv_out),
            ],
            axis=0,
        )
        * scaling
    )
    small_grads = (
        jnp.concatenate(
            [
                jnp.stack([grad_gain_a, grad_gain_s, grad_gain_c, grad_gain_b, grad_gain_out]),
                jnp.stack(kernel_grads),
            ],
            axis=0,
        )
        * scaling
    )
    rows_part = lax.psum_scatter(
        grad_stack.astype(jnp.bfloat16), "rows", scatter_dimension=1, tiled=True
    )
    owned, small_part = (
        lax.psum_scatter(rows_part, "tm", scatter_dimension=0, tiled=True).astype(jnp.float32),
        lax.psum_scatter(
            small_grads.astype(jnp.bfloat16), "tm", scatter_dimension=1, tiled=True
        ).astype(jnp.float32),
    )
    decay_sum, mix_sum, small_sum = lax.psum(
        (grad_logs * scaling, grad_mix_terms * scaling, small_part), "rows"
    )
    full_grad = lax.all_gather(owned.astype(jnp.bfloat16), "rows", axis=1, tiled=True).astype(
        owned.dtype
    )
    slice_rows = owned.shape[1]
    grad_columns = lax.dynamic_slice_in_dim(
        full_grad, lax.axis_index("rows") * slice_rows, slice_rows, 2
    )
    new_left = 0.5 * left_stats + 0.5 * jnp.einsum(
        "bik,bjk->bij", owned, full_grad, precision=precise
    )
    new_right = 0.5 * right_stats + 0.5 * jnp.einsum(
        "bki,bkj->bij", grad_columns, full_grad, precision=precise
    )
    left_side = jnp.einsum("bij,bjk->bik", left_root, full_grad, precision=precise)
    step_value = jnp.einsum("bik,bkl->bil", left_side, right_root, precision=precise)
    new_master = master - rate_blocks * step_value
    small_width = small_sum.shape[1]
    own_small = lax.dynamic_slice_in_dim(
        small_params, lax.axis_index("tm") * small_width, small_width, 1
    )
    new_small = own_small - rate_small * small_sum
    new_decay = decay_logs - rate_small * decay_sum
    new_mix = state_mix - rate_small * mix_sum
    return (
        layer_out.astype(jnp.bfloat16).reshape(row_count, frame_count, width),
        grad_zero.reshape(row_count, frame_count, width),
        grad_state,
        owned,
        new_left,
        new_right,
        new_master,
        new_master.astype(jnp.bfloat16),
        small_sum,
        new_small,
        decay_sum,
        mix_sum,
        new_decay,
        new_mix,
    )


def solution(mesh):
    return jax.shard_map(
        body,
        mesh=mesh,
        in_specs=(
            P("rows", "tm", None),
            P("rows", "tm", None),
            P("rows", "tm", None),
            P("rows"),
            P("tm", "rows", None),
            P("tm", "rows", None),
            P("tm", "rows", None),
            P("tm", "rows", None),
            P("tm", None, None),
            P(),
            P("tm", None),
            P(None, "tm", None),
        ),
        out_specs=(
            P("rows", "tm", None),
            P("rows", "tm", None),
            P("rows", "tm", None),
            P("tm", "rows", None),
            P("tm", "rows", None),
            P("tm", "rows", None),
            P("tm", "rows", None),
            P("tm", "rows", None),
            P(None, "tm"),
            P(None, "tm"),
            P("tm", None),
            P(None, "tm", None),
            P("tm", None),
            P(None, "tm", None),
        ),
        check_vma=False,
    )
```

profile of v0, /device:TPU:0, one launch (start us, length us, event | category | flops | bytes accessed | tf_op | source)
XLA Modules:
  0.0 1053.2 jit_solution(16982755594584130233)
XLA Ops:
  9.4 39.7 %all-gather.4.cloned.1.call-done = bf16[22,256,256]{2,1,0:T(8,128)(2,1)} async-done(((bf16[22,32,256]{2,1,0:T(8,128)(2,1)}), bf16[22,256,256]{2,1,0:T(8,128)(2,1)}) %all-gather.4.cloned.1.call-update) | async-done | bytes 2883600 | tf_op jit(solution)/shard_map/all_gather | solution.py:208
  70.0 26.9 %sine_negate_fusion = (f32[1280,1280]{1,0:T(8,128)S(1)}, f32[1280,1280]{1,0:T(8,128)S(1)}) fusion(), kind=kLoop, calls=%fused_computation.60 | loop fusion | flops 16384000 | bytes 13107200 | tf_op jit(solution)/shard_map/neg | solution.py:119
  111.4 52.3 %all-gather.6.cloned.1.call-done = bf16[88,256,256]{2,1,0:T(8,128)(2,1)} async-done(((bf16[22,256,256]{2,1,0:T(8,128)(2,1)}), bf16[88,256,256]{2,1,0:T(8,128)(2,1)}) %all-gather.6.cloned.1.call-update) | async-done | bytes 11534352 | tf_op jit(solution)/shard_map/all_gather | solution.py:209
  180.0 9.7 multiply_convert_fusion.2
  205.7 28.6 %broadcast_multiply_fusion.1 = (f32[1280,1280]{1,0:T(8,128)}, f32[1280,1280]{1,0:T(8,128)}) fusion(f32[1280]{0:T(1024)S(1)} %select_multiply_fusion), kind=kLoop, calls=%fused_computation.184 | loop fusion | flops 19660800 | bytes 13112320 | tf_op jit(solution)/shard_map/mul | solution.py:119
  246.9 16.8 %fusion.18 = f32[6,128,5120]{2,1,0:T(8,128)} fusion(bf16[6,1280,128]{2,1,0:T(8,128)(2,1)S(1)} %bitcast.422, bf16[1280,2560]{1,0:T(8,128)(2,1)} %subtract_convert_fusion, bf16[1280,2560]{1,0:T(8,128)(2,1)} %fusion.32), kind=kOutput, calls=%fused_computation.49 | convolution fusion | flops 10092544000 | bytes 30801920 | tf_op jit(solution)/shard_map/jvp(rtc,tk->rck)/dot_general | solution.py:145
  276.5 35.6 %fusion.73 = bf16[6,1280,128]{2,1,0:T(8,128)(2,1)S(1)} fusion(f32[6,1280,128]{2,1,0:T(8,128)S(1)} %copy-done.52, f32[6,128,1280]{2,1,0:T(8,128)} %get-tuple-element.127, f32[6,128,1280]{2,1,0:T(8,128)S(1)} %get-tuple-element.126, f32[1280,1280]{1,0:T(8,128)} %get-tuple-element.169, f32[1280,1280]{1,0:T(8,128)} %get-tuple-element.168), kind=kOutput, calls=%fused_computation.136 | convolution fusion | flops 15106703360 | bytes 26869760 | tf_op jit(solution)/shard_map/jvp(rck,kt->rtc)/dot_general | solution.py:163
  330.4 24.2 %all-to-all-done.1 = bf16[6,1280,128]{2,0,1:T(8,128)(2,1)S(1)} async-done(((bf16[6,1280,128]{2,0,1:T(8,128)(2,1)}), bf16[6,1280,128]{2,0,1:T(8,128)(2,1)S(1)}, u32[]{:S(2)}, u32[]{:S(2)}) %all-to-all-start.1) | async-done | bytes 1966112 | tf_op jit(solution)/shard_map/all_to_all | solution.py:234
  407.2 8.8 multiply_convert_fusion.9
  428.0 10.1 multiply_convert_fusion.1
  449.3 14.8 %fusion.2 = bf16[1920,2048]{1,0:T(8,128)(2,1)} fusion(f32[1920,2048]{1,0:T(8,128)} %get-tuple-element.179, bf16[2048,512]{0,1:T(8,128)(2,1)S(1)} %bitcast.412, f32[1920,512]{0,1:T(8,128)S(1)} %get-tuple-element.109, f32[1920]{0:T(1024)S(1)} %negate_multiply_fusion.4), kind=kOutput, calls=%fused_computation.21 | convolution fusion | flops 4068802560 | bytes 29629952 | tf_op jit(solution)/shard_map/dot_general | solution.py:67
  464.1 8.6 multiply_reduce_fusion.5
  560.7 9.6 fusion.120
  570.3 20.0 %all-to-all-done.2 = bf16[6,320,512]{1,0,2:T(8,128)(2,1)} async-done(((bf16[6,320,512]{1,0,2:T(8,128)(2,1)}), bf16[6,320,512]{1,0,2:T(8,128)(2,1)}, u32[]{:S(2)}, u32[]{:S(2)}) %all-to-all-start.2) | async-done | bytes 1966112 | tf_op jit(solution)/shard_map/all_to_all | solution.py:293
  599.4 14.3 %fusion.16 = f32[6,128,2560]{2,1,0:T(8,128)S(1)} fusion(f32[1280,1280]{1,0:T(8,128)} %get-tuple-element.169, f32[1280,1280]{1,0:T(8,128)} %get-tuple-element.168, bf16[6,1280,128]{1,2,0:T(8,128)(2,1)} %copy.214), kind=kOutput, calls=%fused_computation.46 | convolution fusion | flops 15102771200 | bytes 22937600 | tf_op jit(solution)/shard_map/transpose(jvp(rck,kt->rtc))/dot_general | solution.py:163
  623.9 21.3 %fusion.79 = bf16[6,1280,128]{1,2,0:T(8,128)(2,1)S(1)} fusion(bf16[1280,2560]{1,0:T(8,128)(2,1)} %subtract_convert_fusion, bf16[1280,2560]{1,0:T(8,128)(2,1)} %fusion.32, f32[6,128,2560]{2,1,0:T(8,128)} %pad_add_fusion), kind=kOutput, calls=%fused_computation.185 | convolution fusion | flops 10097459200 | bytes 22937600 | tf_op jit(solution)/shard_map/transpose(jvp(rtc,tk->rck))/dot_general | solution.py:145
  703.5 9.7 fusion.187
  723.9 17.8 %fusion.8 = (bf16[2048,1920]{0,1:T(8,128)(2,1)}, f32[1920,2048]{1,0:T(8,128)}) fusion(f32[1920,2048]{1,0:T(8,128)} %get-tuple-element.171, bf16[1920,512]{0,1:T(8,128)(2,1)S(1)} %multiply_convert_fusion.5, bf16[2048,512]{0,1:T(8,128)(2,1)S(1)} %bitcast.407), kind=kOutput, calls=%fused_computation.27 | convolution fusion | flops 4065853440 | bytes 43384832 | tf_op jit(solution)/shard_map/dot_general | solution.py:67
  741.8 10.7 %copy.263 = bf16[2048,1920]{1,0:T(8,128)(2,1)} copy(bf16[2048,1920]{0,1:T(8,128)(2,1)} %get-tuple-element.188) | data formatting | bytes 15728640 | tf_op jit(solution)/shard_map/dot_general | solution.py:61
  752.5 17.1 %multiply_reduce_fusion.9 = (f32[1920]{0:T(1024)S(1)}, f32[1920,512]{0,1:T(8,128)S(1)}) fusion(f32[1920,512]{0,1:T(8,128)} %copy.178, f32[1920]{0:T(1024)S(1)} %copy-done.98, f32[512]{0:T(512)S(1)} %bitcast.439, bf16[512,2048]{1,0:T(8,128)(2,1)S(1)} %bitcast.405, f32[1920,2048]{1,0:T(8,128)} %get-tuple-element.171, f32[1920,2048]{1,0:T(8,128)} %get-tuple-element.189), kind=kOutput, calls=%fused_computation.149 | convolution fusion | flops 4069783552 | bytes 41436160 | tf_op jit(solution)/shard_map/dot_general | solution.py:67
  798.0 120.9 %reduce-scatter.6.cloned.1.call-done = bf16[88,32,256]{2,1,0:T(8,128)(2,1)} async-done(((bf16[88,256,256]{2,1,0:T(8,128)(2,1)}), bf16[88,32,256]{2,1,0:T(8,128)(2,1)}) %reduce-scatter.6.cloned.1.call-update) | async-done | bytes 1441808 | tf_op jit(solution)/shard_map/reduce_scatter | solution.py:336
  919.1 27.1 %fusion.52 = (f32[512]{0:T(512)S(1)}, f32[512]{0:T(512)S(1)}, f32[512]{0:T(512)S(1)}, f32[512]{0:T(512)S(1)}, f32[512]{0:T(512)S(1)}, /*index=5*/f32[512]{0:T(51...) fusion(bf16[6,320,512]{2,1,0:T(8,128)(2,1)S(1)} %bitcast.352, ...), kind=kLoop, calls=%fused_computation.97 | loop fusion | flops 30466560 | bytes 60979200 | tf_op jit(solution)/shard_map/reduce_sum | solution.py:276
  968.7 16.2 %fusion.30 = f32[128,1280]{1,0:T(8,128)S(1)} fusion(f32[1280,1280]{1,0:T(8,128)} %copy-done.2, f32[1280,1280]{1,0:T(8,128)} %copy-done.3, f32[128,1280]{1,0:T(8,128)S(1)} %add_any.121, f32[128,1280]{1,0:T(8,128)S(1)} %add_any.120), kind=kOutput, calls=%fused_computation.66 | convolution fusion | flops 5036769280 | bytes 15073280 | tf_op jit(solution)/shard_map/transpose(jvp())/dot_general | solution.py:144
  998.7 29.4 %all-reduce.13 = (f32[20,128]{1,0:T(8,128)S(1)}, f32[2,32]{1,0:T(2,128)S(1)}, f32[2,128,32]{1,2,0:T(8,128)S(1)}) all-reduce(bf16[20,128]{1,0:T(8,128)(2,1)S(1)} %copy.265, f32[2,32]{1,0:T(2,128)S(1)} %multiply_multiply_fusion.5, f32[2,128,32]{1,2,0:T(8,128)S(1)} %add_multiply_fusion), channel_id=1, replica_groups=mesh['tm'=4,'rows'=8] {'rows'}, use_global_device_ids=true, to_apply=%region_43.44 | all-reduce | flops 10816 | bytes 81408 | tf_op jit(solution)/shard_map/psum | solution.py:345
  (517 shorter events, 446.5 us)
Async XLA Ops:
  7.2 1024.4 %copy-start = (f32[22,32,256]{2,1,0:T(8,128)S(1)}, f32[22,32,256]{2,1,0:T(8,128)}, u32[]{:S(2)}) copy-start(f32[22,32,256]{2,1,0:T(8,128)} %param.19) | copy-start | bytes 2162692
  7.2 42.0 %copy-start.84 = (f32[2,128,32]{1,2,0:T(8,128)S(1)}, f32[2,128,32]{1,2,0:T(8,128)}, u32[]{:S(2)}) copy-start(f32[2,128,32]{1,2,0:T(8,128)} %param.23) | copy-start | bytes 98308
  7.2 42.1 %copy-start.142 = (s32[6]{0:T(128)S(1)}, s32[6]{0:T(128)}, u32[]{:S(2)}) copy-start(s32[6]{0:T(128)} %param.15) | copy-start | bytes 76
  7.2 42.1 %copy-start.88 = (f32[6,128,32]{1,2,0:T(8,128)S(1)}, f32[6,128,32]{1,2,0:T(8,128)}, u32[]{:S(2)}) copy-start(f32[6,128,32]{1,2,0:T(8,128)} %param.14) | copy-start | bytes 294916
  7.2 43.2 %copy-start.26 = (bf16[6,320,512]{2,1,0:T(8,128)(2,1)S(1)}, bf16[6,320,512]{2,1,0:T(8,128)(2,1)}, u32[]{:S(2)}) copy-start(bf16[6,320,512]{2,1,0:T(8,128)(2,1)} %param.12) | copy-start | bytes 5898244
  7.3 41.9 %all-gather.4.cloned.1.call-start = ((), (), s32[]{:S(2)}) async-start(), calls=%async_computation.7 | async-start | bytes 3244032 | tf_op jit(solution)/shard_map/all_gather | solution.py:208
  9.4 154.3 %all-gather.6.cloned.1.call-start = ((), (), s32[]{:S(2)}) async-start(), calls=%async_computation.8 | async-start | bytes 14417920 | tf_op jit(solution)/shard_map/all_gather | solution.py:209
  67.5 127.3 %copy-start.116 = (f32[1,512]{1,0:T(1,128)}, f32[1,512]{1,0:T(1,128)S(1)}, u32[]{:S(2)}) copy-start(f32[1,512]{1,0:T(1,128)S(1)} %get-tuple-element.161) | copy-start | bytes 6148
  67.5 295.0 %copy-start.118 = (f32[1,512]{1,0:T(1,128)}, f32[1,512]{1,0:T(1,128)S(1)}, u32[]{:S(2)}) copy-start(f32[1,512]{1,0:T(1,128)S(1)} %get-tuple-element.159) | copy-start | bytes 6148
  104.9 165.9 %copy-start.45 = (f32[128,1280]{1,0:T(8,128)}, f32[128,1280]{1,0:T(8,128)S(1)}, u32[]{:S(2)}) copy-start(f32[128,1280]{1,0:T(8,128)S(1)} %get-tuple-element.139) | copy-start | bytes 1966084
  200.8 41.2 %all-to-all-start = ((bf16[6,320,512]{1,0,2:T(8,128)(2,1)}), bf16[6,320,512]{1,0,2:T(8,128)(2,1)}, u32[]{:S(2)}, u32[]{:S(2)}) async-start(bf16[6,320,512]{1,0,2:T(8,128)(2,1)} %copy.180), calls=%async_computation | async-start | bytes 6291456 | tf_op jit(solution)/shard_map/all_to_all | solution.py:219
  320.6 34.0 %all-to-all-start.1 = ((bf16[6,1280,128]{2,0,1:T(8,128)(2,1)}), bf16[6,1280,128]{2,0,1:T(8,128)(2,1)S(1)}, u32[]{:S(2)}, u32[]{:S(2)}) async-start(bf16[6,1280,128]{2,0,1:T(8,128)(2,1)} %copy.192), calls=%async_computation.1 | async-start | bytes 5242880 | tf_op jit(solution)/shard_map/all_to_all | solution.py:234
  375.5 30.9 %collective-permute-start = (bf16[6,7,512]{2,1,0:T(8,128)(2,1)}, bf16[6,7,512]{2,1,0:T(8,128)(2,1)S(1)}, u32[]{:S(2)}, u32[]{:S(2)}) collective-permute-start(bf16[6,7,512]{2,1,0:T(8,128)(2,1)} %get-tuple-element.137), channel_id=1, source_target_pairs={{0,8},{8,16},{16,24},{1,9},{9,17},{17,25},{2,10},{10,18},{18,26},{... | collective-permute-start | bytes 129032 | tf_op jit(solution)/shard_map/ppermute | solution.py:24
  378.9 27.6 %collective-permute-start.1 = (bf16[6,7,512]{2,1,0:T(8,128)(2,1)S(1)}, bf16[6,7,512]{2,1,0:T(8,128)(2,1)S(1)}, u32[]{:S(2)}, u32[]{:S(2)}) collective-permute-start(bf16[6,7,512]{2,1,0:T(8,128)(2,1)S(1)} %get-tuple-element.138), channel_id=1, source_target_pairs={{8,0},{16,8},{24,16},{9,1},{17,9},{25,17},{10,2},{18,10},{26,18},{... | collective-permute-start | bytes 129032 | tf_op jit(solution)/shard_map/ppermute | solution.py:27
  425.0 47.8 %copy-start.21 = (f32[1920,512]{0,1:T(8,128)}, f32[1920,512]{0,1:T(8,128)S(1)}, u32[]{:S(2)}) copy-start(f32[1920,512]{0,1:T(8,128)S(1)} %get-tuple-element.177) | copy-start | bytes 11796484
  484.4 17.9 %collective-permute-start.2 = (bf16[6,7,512]{2,1,0:T(8,128)(2,1)S(1)}, bf16[6,7,512]{2,1,0:T(8,128)(2,1)S(1)}, u32[]{:S(2)}, u32[]{:S(2)}) collective-permute-start(bf16[6,7,512]{2,1,0:T(8,128)(2,1)S(1)} %get-tuple-element.135), channel_id=1, source_target_pairs={{0,8},{8,16},{16,24},{1,9},{9,17},{17,25},{2,10},{10,18},{18,26},{... | collective-permute-start | bytes 129032 | tf_op jit(solution)/shard_map/ppermute | solution.py:24
  489.0 13.4 %collective-permute-start.3 = (bf16[6,7,512]{2,1,0:T(8,128)(2,1)S(1)}, bf16[6,7,512]{2,1,0:T(8,128)(2,1)S(1)}, u32[]{:S(2)}, u32[]{:S(2)}) collective-permute-start(bf16[6,7,512]{2,1,0:T(8,128)(2,1)S(1)} %get-tuple-element.136), channel_id=1, source_target_pairs={{8,0},{16,8},{24,16},{9,1},{17,9},{25,17},{10,2},{18,10},{26,18},{... | collective-permute-start | bytes 129032 | tf_op jit(solution)/shard_map/ppermute | solution.py:27
  550.2 40.1 %all-to-all-start.2 = ((bf16[6,320,512]{1,0,2:T(8,128)(2,1)}), bf16[6,320,512]{1,0,2:T(8,128)(2,1)}, u32[]{:S(2)}, u32[]{:S(2)}) async-start(bf16[6,320,512]{1,0,2:T(8,128)(2,1)} %copy.211), calls=%async_computation.2 | async-start | bytes 6291456 | tf_op jit(solution)/shard_map/all_to_all | solution.py:293
  648.6 39.8 %all-to-all-start.3 = ((bf16[6,1280,128]{2,0,1:T(8,128)(2,1)}), bf16[6,1280,128]{2,0,1:T(8,128)(2,1)S(1)}, u32[]{:S(2)}, u32[]{:S(2)}) async-start(bf16[6,1280,128]{2,0,1:T(8,128)(2,1)} %copy.215), calls=%async_computation.3 | async-start | bytes 5242880 | tf_op jit(solution)/shard_map/all_to_all | solution.py:299
  652.4 266.6 %reduce-scatter.6.cloned.1.call-start = ((), (), s32[]{:S(2)}) async-start(), calls=%async_computation.9 | async-start | bytes 12976128 | tf_op jit(solution)/shard_map/reduce_scatter | solution.py:336
  798.0 121.1 %copy-start.29 = (bf16[1920,512]{1,0:T(8,128)(2,1)S(1)}, bf16[1920,512]{1,0:T(8,128)(2,1)}, u32[]{:S(2)}) copy-start(bf16[1920,512]{1,0:T(8,128)(2,1)} %copy-done.28) | copy-start | bytes 5898244
  798.0 152.3 %reduce-scatter.8.cloned.1.call-start = ((), (), s32[]{:S(2)}) async-start(), calls=%async_computation.10 | async-start | bytes 1802240 | tf_op jit(solution)/shard_map/reduce_scatter | solution.py:340
  919.0 78.8 %reduce-scatter.10.cloned.1.call-start = ((), (), s32[]{:S(2)}) async-start(), calls=%async_computation.12 | async-start | bytes 163840
  947.1 84.5 %all-gather.8.cloned.1.call-start = ((), (), s32[]{:S(2)}) async-start(), calls=%async_computation.11 | async-start | bytes 3244032 | tf_op jit(solution)/shard_map/all_gather | solution.py:348
  (143 other events, 1040.9 us)
Sparse Core Ops, SparseCore 0:
  10.3 38.8 all-gather.3
  51.0 112.6 all-gather.5
  798.1 120.7 reduce-scatter.5
  921.7 28.4 reduce-scatter.7
  953.1 23.8 reduce-scatter.9
  978.4 36.6 all-gather.7
where the time goes:
time: 1060 us; the launch traced here: 1050 us
  matrix products  293 us (28%)
  waiting for transfers between devices  268 us (25%)
  local copies, waits for them, and re-layouts  222 us (21%)
  other arithmetic  194 us (18%)
  blocking collectives  29.4 us (3%)
  starting transfers between devices  29.2 us (3%)
  between operations  16.4 us (2%)
    reduce_scatter x1, waiting for transfers between devices, body(): lax.psum_scatter(grad_stack.astype(jnp.bfloat16), 'rows', scatter_dimensi...  121 us
    dot_general x8, matrix products, inner_cols(): lax.dot_general(first, second, (((1,), (1,)), ((), ())), preferred_elemen...  68.7 us
    unnamed x327, local copies, waits for them, and re-layouts  55 us
    all_gather x1, waiting for transfers between devices, body(): block_stack = lax.all_gather(partial_stack, 'tm', axis=0, tiled=True)  52.3 us
    dot_general x2, matrix products, conv_local(): jnp.einsum('rck,kt->rtc', output_hat, inverse_table, precision=three_pass)  49.9 us
    dot_general x8, matrix products, inner_rows(): lax.dot_general(first, second, (((0,), (0,)), ((), ())), preferred_elemen...  46.5 us
    all_gather x1, waiting for transfers between devices, body(): partial_stack = lax.all_gather(copy_part, 'rows', axis=1, tiled=True)  39.7 us
    dot_general x8, matrix products, matmul(): return jnp.dot(first, second, preferred_element_type=jnp.float32)  38.7 us
  transfers between devices with their start and end apart: 14, of which 7 were waited for; matrix products, arithmetic and copies ran while one was open for 25% of the time, Pallas kernels for 0%

commit v1 on v0

--- a/solution.py
+++ b/solution.py
@@ -206,7 +206,14 @@
     scaling = 1.0 / math.sqrt(token_count * lax.axis_size("tm") * lax.axis_size("rows"))
     copy_part = master.astype(jnp.bfloat16)
     partial_stack = lax.all_gather(copy_part, "rows", axis=1, tiled=True)
-    block_stack = lax.all_gather(partial_stack, "tm", axis=0, tiled=True)
+    ways, here, step = (lax.axis_size("tm"), lax.axis_index("tm"), partial_stack.shape[0])
+    line, have = (partial_stack, 1)
+    while have < ways:
+        line = jnp.concatenate(
+            [line, lax.ppermute(line, "tm", [(d, (d - have) % ways) for d in range(ways)])], axis=0
+        )
+        have = 2 * have
+    block_stack = jnp.roll(line, here * step, axis=0)
     ffa_in, ffa_out, ffb_in, ffb_out, mixer_in, mixer_out, conv_in, conv_out = matrices(block_stack)
     kernel_rows = small_params[5:]
     stream_zero = features.astype(jnp.float32).reshape(token_count, width)

time: 1060 us -> 1160 us (1.094)
  waiting for transfers between devices: 268 us -> 326 us
  local copies, waits for them, and re-layouts: 222 us -> 251 us
    ppermute x0 -> x2, waiting for transfers between devices: none -> 113 us  [body(): lax.ppermute(line, 'tm', [(d, (d - have) % ways) for d in range(ways)])]
    all_gather x1 -> x0, waiting for transfers between devices: 52.3 us -> none  [body(): block_stack = lax.all_gather(partial_stack, 'tm', axis=0, tiled=True)]
    unnamed x327 -> x332, local copies, waits for them, and re-layouts: 55 us -> 74.3 us
  transfers between devices with their start and end apart: 14 -> 15, of which waited for: 7 -> 8; matrix products, arithmetic and copies ran while one was open for 25% -> 24% of each run, Pallas kernels for 0% -> 0%
where the time goes in v1:
time: 1160 us; the launch traced here: 1150 us
  waiting for transfers between devices  326 us (28%)
  matrix products  297 us (26%)
  local copies, waits for them, and re-layouts  251 us (22%)
  other arithmetic  200 us (17%)
  starting transfers between devices  33 us (3%)
  blocking collectives  29.3 us (3%)
  between operations  16.1 us (1%)
    reduce_scatter x1, waiting for transfers between devices, body(): lax.psum_scatter(grad_stack.astype(jnp.bfloat16), 'rows', scatter_dimensi...  119 us
    ppermute x2, waiting for transfers between devices, body(): lax.ppermute(line, 'tm', [(d, (d - have) % ways) for d in range(ways)])  113 us
    unnamed x332, local copies, waits for them, and re-layouts  74.3 us
    dot_general x8, matrix products, inner_cols(): lax.dot_general(first, second, (((1,), (1,)), ((), ())), preferred_elemen...  68.9 us
    dot_general x2, matrix products, conv_local(): jnp.einsum('rck,kt->rtc', output_hat, inverse_table, precision=three_pass)  50.1 us
    dot_general x8, matrix products, inner_rows(): lax.dot_general(first, second, (((0,), (0,)), ((), ())), preferred_elemen...  46.7 us
    all_gather x1, waiting for transfers between devices, body(): partial_stack = lax.all_gather(copy_part, 'rows', axis=1, tiled=True)  39.8 us
    dot_general x8, matrix products, matmul(): return jnp.dot(first, second, preferred_element_type=jnp.float32)  38.6 us
  transfers between devices with their start and end apart: 15, of which 8 were waited for; matrix products, arithmetic and copies ran while one was open for 24% of the time, Pallas kernels for 0%

profile of v1, /device:TPU:0, one launch (start us, length us, event | category | flops | bytes accessed | tf_op | source)
XLA Modules:
  0.0 1152.0 jit_solution(14900747077311921334)
XLA Ops:
  9.2 39.8 %all-gather.3.cloned.1.call-done = bf16[22,256,256]{2,1,0:T(8,128)(2,1)} async-done(((bf16[22,32,256]{2,1,0:T(8,128)(2,1)}), bf16[22,256,256]{2,1,0:T(8,128)(2,1)}) %all-gather.3.cloned.1.call-update) | async-done | bytes 2883600 | tf_op jit(solution)/shard_map/all_gather | solution.py:208
  61.6 52.4 %collective-permute-done = bf16[22,256,256]{2,1,0:T(8,128)(2,1)} collective-permute-done((bf16[22,256,256]{2,1,0:T(8,128)(2,1)}, bf16[22,256,256]{2,1,0:T(8,128)(2,1)}, u32[]{:S(2)}, u32[]{:S(2)}) %collective-permute-start) | collective-permute-done | bytes 2883616 | tf_op jit(solution)/shard_map/ppermute | solution.py:213
  137.6 27.1 %sine_negate_fusion = (f32[1280,1280]{1,0:T(8,128)S(1)}, f32[1280,1280]{1,0:T(8,128)S(1)}) fusion(), kind=kLoop, calls=%fused_computation.60 | loop fusion | flops 16384000 | bytes 13107200 | tf_op jit(solution)/shard_map/neg | solution.py:119
  184.5 60.2 %collective-permute-done.1 = bf16[44,256,256]{2,1,0:T(8,128)(2,1)} collective-permute-done((bf16[44,256,256]{2,1,0:T(8,128)(2,1)}, bf16[44,256,256]{2,1,0:T(8,128)(2,1)}, u32[]{:S(2)}, u32[]{:S(2)}) %collective-permute-start.1) | collective-permute-done | bytes 5767200 | tf_op jit(solution)/shard_map/ppermute | solution.py:213
  280.7 9.7 multiply_convert_fusion.2
  306.4 28.6 %broadcast_multiply_fusion.1 = (f32[1280,1280]{1,0:T(8,128)}, f32[1280,1280]{1,0:T(8,128)}) fusion(f32[1280]{0:T(1024)S(1)} %select_multiply_fusion), kind=kLoop, calls=%fused_computation.185 | loop fusion | flops 19660800 | bytes 13112320 | tf_op jit(solution)/shard_map/mul | solution.py:119
  346.9 16.8 %fusion.18 = f32[6,128,5120]{2,1,0:T(8,128)} fusion(bf16[6,1280,128]{2,1,0:T(8,128)(2,1)S(1)} %bitcast.422, bf16[1280,2560]{1,0:T(8,128)(2,1)} %subtract_convert_fusion, bf16[1280,2560]{1,0:T(8,128)(2,1)} %fusion.32), kind=kOutput, calls=%fused_computation.49 | convolution fusion | flops 10092544000 | bytes 30801920 | tf_op jit(solution)/shard_map/jvp(rtc,tk->rck)/dot_general | solution.py:145
  376.6 35.8 %fusion.73 = bf16[6,1280,128]{2,1,0:T(8,128)(2,1)S(1)} fusion(f32[6,1280,128]{2,1,0:T(8,128)S(1)} %copy-done.53, f32[6,128,1280]{2,1,0:T(8,128)} %get-tuple-element.127, f32[6,128,1280]{2,1,0:T(8,128)S(1)} %get-tuple-element.126, f32[1280,1280]{1,0:T(8,128)} %get-tuple-element.169, f32[1280,1280]{1,0:T(8,128)} %get-tuple-element.168), kind=kOutput, calls=%fused_computation.137 | convolution fusion | flops 15106703360 | bytes 26869760 | tf_op jit(solution)/shard_map/jvp(rck,kt->rtc)/dot_general | solution.py:163
  430.4 23.0 %all-to-all-done.1 = bf16[6,1280,128]{2,0,1:T(8,128)(2,1)S(1)} async-done(((bf16[6,1280,128]{2,0,1:T(8,128)(2,1)}), bf16[6,1280,128]{2,0,1:T(8,128)(2,1)S(1)}, u32[]{:S(2)}, u32[]{:S(2)}) %all-to-all-start.1) | async-done | bytes 1966112 | tf_op jit(solution)/shard_map/all_to_all | solution.py:241
  508.5 8.8 multiply_convert_fusion.9
  529.3 10.1 multiply_convert_fusion.1
  550.5 14.8 %fusion.2 = bf16[1920,2048]{1,0:T(8,128)(2,1)} fusion(f32[1920,2048]{1,0:T(8,128)} %get-tuple-element.179, bf16[2048,512]{0,1:T(8,128)(2,1)S(1)} %bitcast.412, f32[1920,512]{0,1:T(8,128)S(1)} %get-tuple-element.109, f32[1920]{0:T(1024)S(1)} %negate_multiply_fusion.4), kind=kOutput, calls=%fused_computation.21 | convolution fusion | flops 4068802560 | bytes 29629952 | tf_op jit(solution)/shard_map/dot_general | solution.py:67
  661.8 9.6 fusion.120
  671.4 19.5 %all-to-all-done.2 = bf16[6,320,512]{1,0,2:T(8,128)(2,1)} async-done(((bf16[6,320,512]{1,0,2:T(8,128)(2,1)}), bf16[6,320,512]{1,0,2:T(8,128)(2,1)}, u32[]{:S(2)}, u32[]{:S(2)}) %all-to-all-start.2) | async-done | bytes 1966112 | tf_op jit(solution)/shard_map/all_to_all | solution.py:300
  700.0 14.3 %fusion.16 = f32[6,128,2560]{2,1,0:T(8,128)S(1)} fusion(f32[1280,1280]{1,0:T(8,128)} %get-tuple-element.169, f32[1280,1280]{1,0:T(8,128)} %get-tuple-element.168, bf16[6,1280,128]{1,2,0:T(8,128)(2,1)} %copy.214), kind=kOutput, calls=%fused_computation.46 | convolution fusion | flops 15102771200 | bytes 22937600 | tf_op jit(solution)/shard_map/transpose(jvp(rck,kt->rtc))/dot_general | solution.py:163
  724.5 21.4 %fusion.79 = bf16[6,1280,128]{1,2,0:T(8,128)(2,1)S(1)} fusion(bf16[1280,2560]{1,0:T(8,128)(2,1)} %subtract_convert_fusion, bf16[1280,2560]{1,0:T(8,128)(2,1)} %fusion.32, f32[6,128,2560]{2,1,0:T(8,128)} %pad_add_fusion), kind=kOutput, calls=%fused_computation.186 | convolution fusion | flops 10097459200 | bytes 22937600 | tf_op jit(solution)/shard_map/transpose(jvp(rtc,tk->rck))/dot_general | solution.py:145
  804.2 9.7 fusion.184
  824.7 17.8 %fusion.8 = (bf16[2048,1920]{0,1:T(8,128)(2,1)}, f32[1920,2048]{1,0:T(8,128)}) fusion(f32[1920,2048]{1,0:T(8,128)} %get-tuple-element.171, bf16[1920,512]{0,1:T(8,128)(2,1)S(1)} %multiply_convert_fusion.5, bf16[2048,512]{0,1:T(8,128)(2,1)S(1)} %bitcast.407), kind=kOutput, calls=%fused_computation.27 | convolution fusion | flops 4065853440 | bytes 43384832 | tf_op jit(solution)/shard_map/dot_general | solution.py:67
  842.5 10.8 copy.263
  853.3 17.3 %multiply_reduce_fusion.9 = (f32[1920]{0:T(1024)S(1)}, f32[1920,512]{0,1:T(8,128)S(1)}) fusion(f32[1920,512]{0,1:T(8,128)} %copy.178, f32[1920]{0:T(1024)S(1)} %copy-done.99, f32[512]{0:T(512)S(1)} %bitcast.439, bf16[512,2048]{1,0:T(8,128)(2,1)S(1)} %bitcast.405, f32[1920,2048]{1,0:T(8,128)} %get-tuple-element.171, f32[1920,2048]{1,0:T(8,128)} %get-tuple-element.189), kind=kOutput, calls=%fused_computation.150 | convolution fusion | flops 4069783552 | bytes 41436160 | tf_op jit(solution)/shard_map/dot_general | solution.py:67
  899.0 118.9 %reduce-scatter.6.cloned.1.call-done = bf16[88,32,256]{2,1,0:T(8,128)(2,1)} async-done(((bf16[88,256,256]{2,1,0:T(8,128)(2,1)}), bf16[88,32,256]{2,1,0:T(8,128)(2,1)}) %reduce-scatter.6.cloned.1.call-update) | async-done | bytes 1441808 | tf_op jit(solution)/shard_map/reduce_scatter | solution.py:343
  1018.1 25.6 %fusion.52 = (f32[512]{0:T(512)S(1)}, f32[512]{0:T(512)S(1)}, f32[512]{0:T(512)S(1)}, f32[512]{0:T(512)S(1)}, f32[512]{0:T(512)S(1)}, /*index=5*/f32[512]{0:T(51...) fusion(bf16[6,320,512]{2,1,0:T(8,128)(2,1)S(1)} %bitcast.352, ...), kind=kLoop, calls=%fused_computation.98 | loop fusion | flops 30466560 | bytes 60979200 | tf_op jit(solution)/shard_map/reduce_sum | solution.py:283
  1067.9 16.2 %fusion.30 = f32[128,1280]{1,0:T(8,128)S(1)} fusion(f32[1280,1280]{1,0:T(8,128)} %copy-done.2, f32[1280,1280]{1,0:T(8,128)} %copy-done.3, f32[128,1280]{1,0:T(8,128)S(1)} %add_any.121, f32[128,1280]{1,0:T(8,128)S(1)} %add_any.120), kind=kOutput, calls=%fused_computation.66 | convolution fusion | flops 5036769280 | bytes 15073280 | tf_op jit(solution)/shard_map/transpose(jvp())/dot_general | solution.py:144
  1097.9 29.3 %all-reduce.13 = (f32[20,128]{1,0:T(8,128)S(1)}, f32[2,32]{1,0:T(2,128)S(1)}, f32[2,128,32]{1,2,0:T(8,128)S(1)}) all-reduce(bf16[20,128]{1,0:T(8,128)(2,1)S(1)} %copy.265, f32[2,32]{1,0:T(2,128)S(1)} %multiply_multiply_fusion.5, f32[2,128,32]{1,2,0:T(8,128)S(1)} %add_multiply_fusion), channel_id=1, replica_groups=mesh['tm'=4,'rows'=8] {'rows'}, use_global_device_ids=true, to_apply=%region_43.44 | all-reduce | flops 10816 | bytes 81408 | tf_op jit(solution)/shard_map/psum | solution.py:352
  (525 shorter events, 498.3 us)
Async XLA Ops:
  7.2 1123.5 %copy-start = (f32[22,32,256]{2,1,0:T(8,128)S(1)}, f32[22,32,256]{2,1,0:T(8,128)}, u32[]{:S(2)}) copy-start(f32[22,32,256]{2,1,0:T(8,128)} %param.19) | copy-start | bytes 2162692
  7.2 41.9 %all-gather.3.cloned.1.call-start = ((), (), s32[]{:S(2)}) async-start(), calls=%async_computation.7 | async-start | bytes 3244032 | tf_op jit(solution)/shard_map/all_gather | solution.py:208
  49.1 64.9 %collective-permute-start = (bf16[22,256,256]{2,1,0:T(8,128)(2,1)}, bf16[22,256,256]{2,1,0:T(8,128)(2,1)}, u32[]{:S(2)}, u32[]{:S(2)}) collective-permute-start(bf16[22,256,256]{2,1,0:T(8,128)(2,1)} %all-gather.3.cloned.1.call-done), channel_id=1, source_target_pairs={{0,24},{8,0},{16,8},{24,16},{1,25},{9,1},{17,9},{25,17},{2,26},{10... | collective-permute-start | bytes 8650760 | tf_op jit(solution)/shard_map/ppermute | solution.py:213
  54.2 59.8 %copy-start.27 = (bf16[22,256,256]{2,1,0:T(8,128)(2,1)S(1)}, bf16[22,256,256]{2,1,0:T(8,128)(2,1)}, u32[]{:S(2)}) copy-start(bf16[22,256,256]{2,1,0:T(8,128)(2,1)} %all-gather.3.cloned.1.call-done) | copy-start | bytes 8650756
  56.3 78.7 %copy-start.115 = (f32[2,32]{1,0:T(2,128)}, f32[2,32]{1,0:T(2,128)S(1)}, u32[]{:S(2)}) copy-start(f32[2,32]{1,0:T(2,128)S(1)} %exponential_negate_fusion) | copy-start | bytes 772
  56.4 79.4 %copy-start.88 = (f32[6,320]{1,0:T(8,128)}, f32[6,320]{1,0:T(8,128)S(1)}, u32[]{:S(2)}) copy-start(f32[6,320]{1,0:T(8,128)S(1)} %broadcast_multiply_fusion.3) | copy-start | bytes 23044
  61.6 58.6 %copy-start.26 = (bf16[6,320,512]{2,1,0:T(8,128)(2,1)S(1)}, bf16[6,320,512]{2,1,0:T(8,128)(2,1)}, u32[]{:S(2)}) copy-start(bf16[6,320,512]{2,1,0:T(8,128)(2,1)} %param.12) | copy-start | bytes 5898244
  61.6 59.5 %copy-start.107 = (f32[20,512]{1,0:T(8,128)S(1)}, f32[20,512]{1,0:T(8,128)}, u32[]{:S(2)}) copy-start(f32[20,512]{1,0:T(8,128)} %param.21) | copy-start | bytes 122884
  118.8 125.9 %collective-permute-start.1 = (bf16[44,256,256]{2,1,0:T(8,128)(2,1)}, bf16[44,256,256]{2,1,0:T(8,128)(2,1)}, u32[]{:S(2)}, u32[]{:S(2)}) collective-permute-start(bf16[44,256,256]{2,1,0:T(8,128)(2,1)} %pad_maximum_fusion.3), channel_id=1, source_target_pairs={{0,16},{8,24},{16,0},{24,8},{1,17},{9,25},{17,1},{25,9},{2,18},{10... | collective-permute-start | bytes 17301512 | tf_op jit(solution)/shard_map/ppermute | solution.py:213
  135.0 160.4 %copy-start.117 = (f32[1,512]{1,0:T(1,128)}, f32[1,512]{1,0:T(1,128)S(1)}, u32[]{:S(2)}) copy-start(f32[1,512]{1,0:T(1,128)S(1)} %get-tuple-element.161) | copy-start | bytes 6148
  172.6 198.3 %copy-start.46 = (f32[128,1280]{1,0:T(8,128)}, f32[128,1280]{1,0:T(8,128)S(1)}, u32[]{:S(2)}) copy-start(f32[128,1280]{1,0:T(8,128)S(1)} %get-tuple-element.139) | copy-start | bytes 1966084
  301.5 40.6 %all-to-all-start = ((bf16[6,320,512]{1,0,2:T(8,128)(2,1)}), bf16[6,320,512]{1,0,2:T(8,128)(2,1)}, u32[]{:S(2)}, u32[]{:S(2)}) async-start(bf16[6,320,512]{1,0,2:T(8,128)(2,1)} %copy.180), calls=%async_computation | async-start | bytes 6291456 | tf_op jit(solution)/shard_map/all_to_all | solution.py:226
  420.9 32.6 %all-to-all-start.1 = ((bf16[6,1280,128]{2,0,1:T(8,128)(2,1)}), bf16[6,1280,128]{2,0,1:T(8,128)(2,1)S(1)}, u32[]{:S(2)}, u32[]{:S(2)}) async-start(bf16[6,1280,128]{2,0,1:T(8,128)(2,1)} %copy.192), calls=%async_computation.1 | async-start | bytes 5242880 | tf_op jit(solution)/shard_map/all_to_all | solution.py:241
  473.8 33.8 %collective-permute-start.2 = (bf16[6,7,512]{2,1,0:T(8,128)(2,1)S(1)}, bf16[6,7,512]{2,1,0:T(8,128)(2,1)S(1)}, u32[]{:S(2)}, u32[]{:S(2)}) collective-permute-start(bf16[6,7,512]{2,1,0:T(8,128)(2,1)S(1)} %get-tuple-element.137), channel_id=1, source_target_pairs={{0,8},{8,16},{16,24},{1,9},{9,17},{17,25},{2,10},{10,18},{18,26},{... | collective-permute-start | bytes 129032 | tf_op jit(solution)/shard_map/ppermute | solution.py:24
  477.3 30.3 %collective-permute-start.3 = (bf16[6,7,512]{2,1,0:T(8,128)(2,1)S(1)}, bf16[6,7,512]{2,1,0:T(8,128)(2,1)S(1)}, u32[]{:S(2)}, u32[]{:S(2)}) collective-permute-start(bf16[6,7,512]{2,1,0:T(8,128)(2,1)S(1)} %get-tuple-element.138), channel_id=1, source_target_pairs={{8,0},{16,8},{24,16},{9,1},{17,9},{25,17},{10,2},{18,10},{26,18},{... | collective-permute-start | bytes 129032 | tf_op jit(solution)/shard_map/ppermute | solution.py:27
  585.6 17.9 %collective-permute-start.4 = (bf16[6,7,512]{2,1,0:T(8,128)(2,1)S(1)}, bf16[6,7,512]{2,1,0:T(8,128)(2,1)S(1)}, u32[]{:S(2)}, u32[]{:S(2)}) collective-permute-start(bf16[6,7,512]{2,1,0:T(8,128)(2,1)S(1)} %get-tuple-element.135), channel_id=1, source_target_pairs={{0,8},{8,16},{16,24},{1,9},{9,17},{17,25},{2,10},{10,18},{18,26},{... | collective-permute-start | bytes 129032 | tf_op jit(solution)/shard_map/ppermute | solution.py:24
  590.2 13.4 %collective-permute-start.5 = (bf16[6,7,512]{2,1,0:T(8,128)(2,1)S(1)}, bf16[6,7,512]{2,1,0:T(8,128)(2,1)S(1)}, u32[]{:S(2)}, u32[]{:S(2)}) collective-permute-start(bf16[6,7,512]{2,1,0:T(8,128)(2,1)S(1)} %get-tuple-element.136), channel_id=1, source_target_pairs={{8,0},{16,8},{24,16},{9,1},{17,9},{25,17},{10,2},{18,10},{26,18},{... | collective-permute-start | bytes 129032 | tf_op jit(solution)/shard_map/ppermute | solution.py:27
  651.4 39.4 %all-to-all-start.2 = ((bf16[6,320,512]{1,0,2:T(8,128)(2,1)}), bf16[6,320,512]{1,0,2:T(8,128)(2,1)}, u32[]{:S(2)}, u32[]{:S(2)}) async-start(bf16[6,320,512]{1,0,2:T(8,128)(2,1)} %copy.211), calls=%async_computation.2 | async-start | bytes 6291456 | tf_op jit(solution)/shard_map/all_to_all | solution.py:300
  749.3 39.9 %all-to-all-start.3 = ((bf16[6,1280,128]{2,0,1:T(8,128)(2,1)}), bf16[6,1280,128]{2,0,1:T(8,128)(2,1)S(1)}, u32[]{:S(2)}, u32[]{:S(2)}) async-start(bf16[6,1280,128]{2,0,1:T(8,128)(2,1)} %copy.215), calls=%async_computation.3 | async-start | bytes 5242880 | tf_op jit(solution)/shard_map/all_to_all | solution.py:306
  753.1 264.9 %reduce-scatter.6.cloned.1.call-start = ((), (), s32[]{:S(2)}) async-start(), calls=%async_computation.8 | async-start | bytes 12976128 | tf_op jit(solution)/shard_map/reduce_scatter | solution.py:343
  899.0 119.1 %copy-start.31 = (bf16[1920,512]{1,0:T(8,128)(2,1)S(1)}, bf16[1920,512]{1,0:T(8,128)(2,1)}, u32[]{:S(2)}) copy-start(bf16[1920,512]{1,0:T(8,128)(2,1)} %copy-done.30) | copy-start | bytes 5898244
  899.0 150.4 %reduce-scatter.8.cloned.1.call-start = ((), (), s32[]{:S(2)}) async-start(), calls=%async_computation.9 | async-start | bytes 1802240 | tf_op jit(solution)/shard_map/reduce_scatter | solution.py:347
  1018.0 78.9 %reduce-scatter.10.cloned.1.call-start = ((), (), s32[]{:S(2)}) async-start(), calls=%async_computation.11 | async-start | bytes 163840
  1044.7 86.0 %all-gather.5.cloned.1.call-start = ((), (), s32[]{:S(2)}) async-start(), calls=%async_computation.10 | async-start | bytes 3244032 | tf_op jit(solution)/shard_map/all_gather | solution.py:355
  (144 other events, 1074.2 us)
Sparse Core Ops, SparseCore 0:
  10.2 38.8 all-gather.2
  899.1 118.8 reduce-scatter.5
  1020.9 28.4 reduce-scatter.7
  1052.2 23.8 reduce-scatter.9
  1077.5 36.6 all-gather.4
